TPU v7x, 128 devices: a whole 4x4x4 slice. The times are simulated.
128 devices in a mesh: grp: 4 (over x), mem: 32 (over z, y, core).
Axes of the slice: x: 4, y: 4, z: 4, core: 2. Of those that a mesh axis runs over, the one named last changes fastest.
Arguments:
- embeddings: bfloat16 [16384, 1024], P(('grp', 'mem')), may hold values from -6 to 6
- cluster: int32 [16384, 1], P(('grp', 'mem')), may hold values from 0 to 3; in each aligned block of 128 rows (0 to 127, 128 to 255, ...) at most 64 rows name the same one
- rank: int32 [16384], P(('grp', 'mem')), may hold values from 0 to 1048575
Outputs:
- similarity: float32 [16384], P(('grp', 'mem'))
Inputs may be any that keep to these rules, and one draw needn't show every extreme that they name: `cluster`: in each aligned block of 128 rows (the rows of one device) no group is named by more than 64 rows. A smaller rank is earlier; equal ranks are not earlier.
All inputs are finite; a program needn't handle non-finite values.
Results may differ from a plain program's by a relative error of at most 0.0013.
Values may be sent and summed in bfloat16 or wider, within the bound.
A program may use at most 64 MiB of HBM per device.

v0:
```python
import jax
import jax.numpy as jnp
from jax import lax
from jax.sharding import PartitionSpec as P

absent_rank = 1073741824


def block_gram(queries, others):
    return lax.dot_general(
        queries, others, (((1,), (1,)), ((), ())), preferred_element_type=jnp.float32
    )


def row_maxima(gram, query_rank, other_rank):
    earlier = other_rank[None, :] < query_rank[:, None]
    return jnp.max(jnp.where(earlier, gram, jnp.float32(-1.0)), axis=1)


def body(embeddings, cluster, rank):
    rows = embeddings.shape[0]
    width = embeddings.shape[1]
    groups = lax.axis_size("grp")
    capacity = max(2, 2 * rows // groups)
    slots = groups * capacity
    wide = embeddings.astype(jnp.float32)
    normed = (wide * lax.rsqrt(jnp.sum(wide * wide, axis=1, keepdims=True) + 1e-06)).astype(
        jnp.bfloat16
    )
    owner = cluster[:, 0]
    onehot = (owner[:, None] == jnp.arange(groups, dtype=jnp.int32)[None, :]).astype(jnp.int32)
    before = jnp.cumsum(onehot, axis=0) - onehot
    position = jnp.sum(before * onehot, axis=1)
    slot = owner * capacity + position
    outgoing = jnp.zeros((slots, width), jnp.bfloat16).at[slot].set(normed)
    out_rank = jnp.full((slots,), absent_rank, jnp.int32).at[slot].set(rank)
    keys, key_rank = (
        lax.all_to_all(outgoing, "grp", split_axis=0, concat_axis=0, tiled=True),
        lax.all_to_all(out_rank, "grp", split_axis=0, concat_axis=0, tiled=True),
    )
    gram = block_gram(keys, lax.all_gather(keys, "mem", axis=0, tiled=True))
    best = jnp.maximum(
        jnp.full((slots,), -1.0, jnp.float32),
        row_maxima(gram, key_rank, lax.all_gather(key_rank, "mem", axis=0, tiled=True)),
    )
    home = lax.all_to_all(best, "grp", split_axis=0, concat_axis=0, tiled=True)
    return home[slot]


def solution(mesh):
    in_specs = (P(("grp", "mem"), None), P(("grp", "mem"), None), P(("grp", "mem")))
    out_specs = P(("grp", "mem"))
    return jax.shard_map(body, mesh=mesh, in_specs=in_specs, out_specs=out_specs, check_vma=False)
```

profile of v0, /device:TPU:0, one launch (start us, length us, event | category | flops | bytes accessed | tf_op | source)
XLA Modules:
  0.0 129.6 jit_solution(2143554724468487378)
XLA Ops:
  6.5 0.0 all-gather.3.cloned.1.call-start
  6.5 0.7 fusion.7
  7.3 0.2 reduce_window_sum.11
  7.5 0.8 select_reduce_fusion
  8.3 0.7 fusion.8
  9.0 1.1 fusion.1
  10.0 1.8 %scatter_custom_fusion.1 = bf16[256,1024]{1,0:T(8,128)(2,1)S(1)} fusion(s32[128]{0:T(128)S(1)} %fusion.8, bf16[128,1024]{1,0:T(8,128)(2,1)} %param.3, f32[128]{0:T(128)S(1)} %add_rsqrt_fusion, bf16[]{:T(256)} %constant.4.clone.1), kind=kCustom, calls=%fused_computation.9 | custom fusion | flops 393216 | bytes 786946 | tf_op jit(solution)/shard_map/scatter | solution.py:35
  11.8 13.8 %all_to_all.33 = bf16[4,64,1024]{2,1,0:T(8,128)(2,1)} all-to-all(bf16[4,64,1024]{2,1,0:T(8,128)(2,1)S(1)} %bitcast.19), channel_id=1, replica_groups=mesh['grp'=4,'mem'=32] {'grp'}, dimensions={0} | all-to-all | bytes 1048576 | tf_op jit(solution)/shard_map/all_to_all | solution.py:38
  25.6 0.0 all-gather.3.cloned.1.call-update
  25.7 1.1 scatter_custom_fusion
  26.8 0.1 all_to_all.22
  26.9 7.6 %all_to_all.34 = s32[4,64,1]{1,2,0:T(1,128)S(1)} all-to-all(s32[4,64,1]{1,2,0:T(1,128)S(1)} %bitcast.22), channel_id=1, replica_groups=mesh['grp'=4,'mem'=32] {'grp'}, dimensions={0} | all-to-all | bytes 2048 | tf_op jit(solution)/shard_map/all_to_all | solution.py:39
  34.5 0.1 all_to_all.24
  34.5 0.5 broadcast.45
  35.1 0.7 reduce.8
  35.7 0.1 reshape.52
  35.8 25.8 %all-gather = s32[32,1,256]{2,1,0:T(1,128)S(1)} all-gather(s32[1,1,256]{2,1,0:T(1,128)S(1)} %reshape.52), channel_id=1, replica_groups=mesh['grp'=4,'mem'=32] {'mem'}, dimensions={0}, use_global_device_ids=true | all-gather | bytes 33792 | tf_op jit(solution)/shard_map/all_gather | solution.py:44
  61.6 37.4 %all-gather.3.cloned.1.call-done = bf16[8192,1024]{1,0:T(8,128)(2,1)} async-done(((bf16[256,1024]{1,0:T(8,128)(2,1)}), bf16[8192,1024]{1,0:T(8,128)(2,1)}) %all-gather.3.cloned.1.call-update) | async-done | bytes 16777232 | tf_op jit(solution)/shard_map/all_gather | solution.py:41
  99.0 10.6 %fusion = f32[256]{0:T(256)S(1)} fusion(bf16[256,1024]{1,0:T(8,128)(2,1)} %bitcast.18, bf16[8192,1024]{1,0:T(8,128)(2,1)} %all-gather.3.cloned.1.call-done, s32[256]{0:T(256)S(1)} %all_to_all.24, s32[8192]{0:T(1024)S(1)} %bitcast.20), kind=kOutput, calls=%fused_computation.4 | convolution fusion | flops 4301258752 | bytes 17336320 | tf_op jit(solution)/shard_map/dot_general | solution.py:10
  109.7 0.7 max_broadcast_in_dim.14
  110.3 4.2 %all-to-all-start.2 = ((f32[4,64,1]{1,2,0:T(1,128)}), f32[4,64,1]{1,2,0:T(1,128)S(1)}, u32[]{:S(2)}, u32[]{:S(2)}) async-start(f32[4,64,1]{1,2,0:T(1,128)} %bitcast.7), calls=%async_computation.2 | async-start | bytes 4096 | tf_op jit(solution)/shard_map/all_to_all | solution.py:46
  114.6 5.1 %all-to-all-done.2 = f32[4,64,1]{1,2,0:T(1,128)S(1)} async-done(((f32[4,64,1]{1,2,0:T(1,128)}), f32[4,64,1]{1,2,0:T(1,128)S(1)}, u32[]{:S(2)}, u32[]{:S(2)}) %all-to-all-start.2) | async-done | bytes 1056 | tf_op jit(solution)/shard_map/all_to_all | solution.py:46
  119.7 0.5 broadcast.46
  120.2 0.7 reduce.9
  120.9 0.1 all_to_all.29
  121.0 1.8 %gather_fusion = f32[128]{0:T(128)} fusion(f32[256]{0:T(256)S(1)} %all_to_all.29, s32[1024]{0:T(1024)S(1)} %pad_clamp_fusion), kind=kCustom, calls=%fused_computation | custom fusion | bytes 1536 | tf_op jit(solution)/shard_map/gather | solution.py:47
  (3 shorter events, 0.0 us)
Async XLA Ops:
  6.5 92.5 %all-gather.3.cloned.1.call-start = ((), (), s32[]{:S(2)}) async-start(), calls=%async_computation.3 | async-start | bytes 17301504 | tf_op jit(solution)/shard_map/all_gather | solution.py:41
  110.3 9.4 %all-to-all-start.2 = ((f32[4,64,1]{1,2,0:T(1,128)}), f32[4,64,1]{1,2,0:T(1,128)S(1)}, u32[]{:S(2)}, u32[]{:S(2)}) async-start(f32[4,64,1]{1,2,0:T(1,128)} %bitcast.7), calls=%async_computation.2 | async-start | bytes 4096 | tf_op jit(solution)/shard_map/all_to_all | solution.py:46
Sparse Core Ops, SparseCore 0:
  25.8 73.2 all-gather.2
where the time goes:
time: 130 us
  blocking collectives  47.2 us (36%)
  waiting for transfers between devices  42.5 us (33%)
  between operations  13.4 us (10%)
  matrix products  10.6 us (8%)
  other arithmetic  6.62 us (5%)
  local copies, waits for them, and re-layouts  4.9 us (4%)
  starting transfers between devices  4.25 us (3%)
    all_gather x1, waiting for transfers between devices, body(): gram = block_gram(keys, lax.all_gather(keys, 'mem', axis=0, tiled=True))  37.4 us
    all_gather x1, blocking collectives, body(): lax.all_gather(key_rank, 'mem', axis=0, tiled=True)  25.8 us
    all_to_all x1, blocking collectives, body(): lax.all_to_all(outgoing, 'grp', split_axis=0, concat_axis=0, tiled=True)  13.8 us
    dot_general x1, matrix products, block_gram(): lax.dot_general(queries, others, (((1,), (1,)), ((), ())), preferred_elem...  10.6 us
    all_to_all x1, blocking collectives, body(): lax.all_to_all(out_rank, 'grp', split_axis=0, concat_axis=0, tiled=True)  7.61 us
    all_to_all x1, waiting for transfers between devices, body(): home = lax.all_to_all(best, 'grp', split_axis=0, concat_axis=0, tiled=True)  5.12 us
    all_to_all x1, starting transfers between devices, body(): home = lax.all_to_all(best, 'grp', split_axis=0, concat_axis=0, tiled=True)  4.25 us
  transfers between devices with their start and end apart: 2, of which 2 were waited for; matrix products, arithmetic and copies ran while one was open for 2% of the time, Pallas kernels for 0%

commit v1 on v0

--- a/solution.py
+++ b/solution.py
@@ -4,6 +4,12 @@
 from jax.sharding import PartitionSpec as P
 
 absent_rank = 1073741824
+
+
+def _supply_all_types(local_values, axis_name):
+    side_arr = jnp.concatenate([local_values] * lax.axis_size(axis_name), axis=0)
+    lower = lax.all_to_all(side_arr, axis_name=axis_name, split_axis=0, concat_axis=0, tiled=True)
+    return lower
 
 
 def block_gram(queries, others):
@@ -41,7 +47,7 @@
     gram = block_gram(keys, lax.all_gather(keys, "mem", axis=0, tiled=True))
     best = jnp.maximum(
         jnp.full((slots,), -1.0, jnp.float32),
-        row_maxima(gram, key_rank, lax.all_gather(key_rank, "mem", axis=0, tiled=True)),
+        row_maxima(gram, key_rank, _supply_all_types(key_rank, "mem")),
     )
     home = lax.all_to_all(best, "grp", split_axis=0, concat_axis=0, tiled=True)
     return home[slot]

time: 130 us -> 130 us (level)
  waiting for transfers between devices: 42.5 us -> 53.1 us
  blocking collectives: 47.2 us -> 37 us
    all_gather x1 -> x0, blocking collectives: 25.8 us -> none  [body(): lax.all_gather(key_rank, 'mem', axis=0, tiled=True)]
    all_to_all x0 -> x1, blocking collectives: none -> 15.6 us  [_supply_all_types(): lax.all_to_all(side_arr, axis_name=axis_name, split_axis=0, concat_axis=0...]
    all_gather x1, waiting for transfers between devices: 37.4 us -> 48 us  [body(): gram = block_gram(keys, lax.all_gather(keys, 'mem', axis=0, tiled=True))]
where the time goes in v1:
time: 130 us
  waiting for transfers between devices  53.1 us (41%)
  blocking collectives  37 us (28%)
  between operations  13.4 us (10%)
  matrix products  10.6 us (8%)
  other arithmetic  6.62 us (5%)
  local copies, waits for them, and re-layouts  4.84 us (4%)
  starting transfers between devices  4.25 us (3%)
    all_gather x1, waiting for transfers between devices, body(): gram = block_gram(keys, lax.all_gather(keys, 'mem', axis=0, tiled=True))  48 us
    all_to_all x1, blocking collectives, _supply_all_types(): lax.all_to_all(side_arr, axis_name=axis_name, split_axis=0, concat_axis=0...  15.6 us
    all_to_all x1, blocking collectives, body(): lax.all_to_all(outgoing, 'grp', split_axis=0, concat_axis=0, tiled=True)  13.8 us
    dot_general x1, matrix products, block_gram(): lax.dot_general(queries, others, (((1,), (1,)), ((), ())), preferred_elem...  10.6 us
    all_to_all x1, blocking collectives, body(): lax.all_to_all(out_rank, 'grp', split_axis=0, concat_axis=0, tiled=True)  7.61 us
    all_to_all x1, waiting for transfers between devices, body(): home = lax.all_to_all(best, 'grp', split_axis=0, concat_axis=0, tiled=True)  5.12 us
    all_to_all x1, starting transfers between devices, body(): home = lax.all_to_all(best, 'grp', split_axis=0, concat_axis=0, tiled=True)  4.25 us
  transfers between devices with their start and end apart: 2, of which 2 were waited for; matrix products, arithmetic and copies ran while one was open for 2% of the time, Pallas kernels for 0%

profile of v1, /device:TPU:0, one launch (start us, length us, event | category | flops | bytes accessed | tf_op | source)
XLA Modules:
  0.0 129.9 jit_solution(9420239891254407428)
XLA Ops:
  6.5 0.0 all-gather.2.cloned.1.call-start
  6.5 1.1 fusion.1
  7.6 0.7 fusion.7
  8.4 0.2 reduce_window_sum.11
  8.6 0.8 select_reduce_fusion
  9.4 0.7 fusion.8
  10.1 1.8 %scatter_custom_fusion.1 = bf16[256,1024]{1,0:T(8,128)(2,1)S(1)} fusion(s32[128]{0:T(128)S(1)} %fusion.8, bf16[128,1024]{1,0:T(8,128)(2,1)} %param.3, f32[128]{0:T(128)S(1)} %add_rsqrt_fusion, bf16[]{:T(256)} %constant.4.clone.1), kind=kCustom, calls=%fused_computation.9 | custom fusion | flops 393216 | bytes 786946 | tf_op jit(solution)/shard_map/scatter | solution.py:41
  11.8 13.8 %all_to_all.36 = bf16[4,64,1024]{2,1,0:T(8,128)(2,1)} all-to-all(bf16[4,64,1024]{2,1,0:T(8,128)(2,1)S(1)} %bitcast.20), channel_id=1, replica_groups=mesh['grp'=4,'mem'=32] {'grp'}, dimensions={0} | all-to-all | bytes 1048576 | tf_op jit(solution)/shard_map/all_to_all | solution.py:44
  25.6 0.0 all-gather.2.cloned.1.call-update
  25.7 1.1 scatter_custom_fusion
  26.8 0.1 all_to_all.24
  26.9 7.6 %all_to_all.37 = s32[4,64,1]{1,2,0:T(1,128)S(1)} all-to-all(s32[4,64,1]{1,2,0:T(1,128)S(1)} %bitcast.22), channel_id=1, replica_groups=mesh['grp'=4,'mem'=32] {'grp'}, dimensions={0} | all-to-all | bytes 2048 | tf_op jit(solution)/shard_map/all_to_all | solution.py:45
  34.5 0.5 broadcast.44
  35.0 0.7 reduce.6
  35.6 0.1 concatenate.6
  35.8 15.6 %all_to_all.38 = s32[32,256,1]{1,2,0:T(1,128)S(1)} all-to-all(s32[32,256,1]{1,2,0:T(1,128)S(1)} %concatenate.7), channel_id=1, replica_groups=mesh['grp'=4,'mem'=32] {'mem'}, dimensions={0} | all-to-all | bytes 65536 | tf_op jit(solution)/shard_map/all_to_all | solution.py:11
  51.4 48.0 %all-gather.2.cloned.1.call-done = bf16[8192,1024]{1,0:T(8,128)(2,1)} async-done(((bf16[256,1024]{1,0:T(8,128)(2,1)}), bf16[8192,1024]{1,0:T(8,128)(2,1)}) %all-gather.2.cloned.1.call-update) | async-done | bytes 16777232 | tf_op jit(solution)/shard_map/all_gather | solution.py:47
  99.3 10.6 %fusion = f32[256]{0:T(256)S(1)} fusion(bf16[256,1024]{1,0:T(8,128)(2,1)} %bitcast.19, bf16[8192,1024]{1,0:T(8,128)(2,1)} %all-gather.2.cloned.1.call-done, s32[256]{0:T(256)S(1)} %concatenate.6, s32[8192]{0:T(1024)S(1)} %bitcast.21), kind=kOutput, calls=%fused_computation.4 | convolution fusion | flops 4301258752 | bytes 17336320 | tf_op jit(solution)/shard_map/dot_general | solution.py:16
  110.0 0.7 max_broadcast_in_dim.14
  110.7 4.2 %all-to-all-start.3 = ((f32[4,64,1]{1,2,0:T(1,128)}), f32[4,64,1]{1,2,0:T(1,128)S(1)}, u32[]{:S(2)}, u32[]{:S(2)}) async-start(f32[4,64,1]{1,2,0:T(1,128)} %bitcast.7), calls=%async_computation.3 | async-start | bytes 4096 | tf_op jit(solution)/shard_map/all_to_all | solution.py:52
  114.9 5.1 %all-to-all-done.3 = f32[4,64,1]{1,2,0:T(1,128)S(1)} async-done(((f32[4,64,1]{1,2,0:T(1,128)}), f32[4,64,1]{1,2,0:T(1,128)S(1)}, u32[]{:S(2)}, u32[]{:S(2)}) %all-to-all-start.3) | async-done | bytes 1056 | tf_op jit(solution)/shard_map/all_to_all | solution.py:52
  120.0 0.5 broadcast.45
  120.5 0.7 reduce.7
  121.2 0.1 all_to_all.31
  121.3 1.8 %gather_fusion = f32[128]{0:T(128)} fusion(f32[256]{0:T(256)S(1)} %all_to_all.31, s32[1024]{0:T(1024)S(1)} %pad_clamp_fusion), kind=kCustom, calls=%fused_computation | custom fusion | bytes 1536 | tf_op jit(solution)/shard_map/gather | solution.py:53
  (4 shorter events, 0.0 us)
Async XLA Ops:
  6.5 92.8 %all-gather.2.cloned.1.call-start = ((), (), s32[]{:S(2)}) async-start(), calls=%async_computation.4 | async-start | bytes 17301504 | tf_op jit(solution)/shard_map/all_gather | solution.py:47
  110.7 9.4 %all-to-all-start.3 = ((f32[4,64,1]{1,2,0:T(1,128)}), f32[4,64,1]{1,2,0:T(1,128)S(1)}, u32[]{:S(2)}, u32[]{:S(2)}) async-start(f32[4,64,1]{1,2,0:T(1,128)} %bitcast.7), calls=%async_computation.3 | async-start | bytes 4096 | tf_op jit(solution)/shard_map/all_to_all | solution.py:52
Sparse Core Ops, SparseCore 0:
  25.8 73.5 all-gather.1
